TPU v7x, 512 devices: a whole 4x4x16 slice. The times are simulated.
512 devices in a mesh: dp: 32 (over z, core), mp: 16 (over x, y).
Axes of the slice: x: 4, y: 4, z: 16, core: 2. Of those that a mesh axis runs over, the one named last changes fastest.
Arguments:
- hidden_in: bfloat16 [64, 512, 8192], P('dp', None, 'mp'), may hold values from -6 to 6
- query_act: bfloat16 [64, 512, 8192], P('dp', None, 'mp'), may hold values from -6 to 6
- key_act: bfloat16 [64, 512, 1024], P('dp'), may hold values from -6 to 6
- value_act: bfloat16 [64, 512, 1024], P('dp'), may hold values from -6 to 6
- ctx_grad: bfloat16 [64, 512, 8192], P('dp', None, 'mp'), may hold values from -6 to 6
- segment_ids: int32 [64, 512], P('dp'), may hold values from 0 to 3, never falling along the last dimension, each value on 1 to 256 neighbouring positions
- down_query: bfloat16 [8192, 128], P('mp'), may hold values from -0.0625 to 0.0625
- up_query: bfloat16 [128, 8192], P(None, 'mp'), may hold values from -0.5 to 0.5
- down_value: bfloat16 [8192, 128], P('mp'), may hold values from -0.0625 to 0.0625
- up_value: bfloat16 [128, 1024], replicated, may hold values from -0.5 to 0.5
- block_rows: int32 [3, 8192], P(None, 'mp'), may hold values from 0 to 63
- tile_rows: int32 [3, 8192], P(None, 'mp'), may hold values from 0 to 7
- block_value: int32 [1024], replicated, may hold values from 0 to 63
- tile_value: int32 [1024], replicated, may hold values from 0 to 7
- tile_bank: bfloat16 [8, 128, 128], replicated, may hold values from -0.5 to 0.5
- seed_feats: bfloat16 [1024, 8192], P('dp', 'mp'), may hold values from -6 to 6
Outputs:
- scores: float32 [64, 1024], P('dp', 'mp')
All inputs are finite; a program needn't handle non-finite values.
Results may differ from a plain program's by a relative error of at most 0.022.
Values may be sent and summed in bfloat16 or wider, within the bound.
No kernel may reach another device: no remote copies, remote signals or barrier semaphores. Data moves between devices by JAX's collectives and lax.ppermute only.
A program may use at most 64 MiB of HBM per device.

v0:
```python
import math
import jax
import jax.numpy as jnp
from jax import lax
from jax.sharding import PartitionSpec as P

H = 64
KVH = 8
DH = 128
R = 128
K = 8192
PB = 128
NT = 8
EPS = 1e-06


def local(
    hidden_in,
    query_act,
    key_act,
    value_act,
    ctx_grad,
    segment_ids,
    down_query,
    up_query,
    down_value,
    up_value,
    block_rows,
    tile_rows,
    block_value,
    tile_value,
    tile_bank,
    seed_feats,
):
    model_index = lax.axis_index("mp")
    cand_count, seq_len, width_dev = query_act.shape
    heads_dev = width_dev // DH
    head_group = H // KVH
    kv_count = max(heads_dev // head_group, 1)
    repeats = heads_dev // kv_count
    kv_first = model_index * heads_dev // head_group
    kv_width = kv_count * DH
    key_local = lax.dynamic_slice_in_dim(key_act, kv_first * DH, kv_width, 2)
    value_local = lax.dynamic_slice_in_dim(value_act, kv_first * DH, kv_width, 2)
    up_local = lax.dynamic_slice_in_dim(up_value, kv_first * DH, kv_width, 1)
    block_local = lax.dynamic_slice_in_dim(block_value, kv_first * DH, kv_width, 0)
    tile_local = lax.dynamic_slice_in_dim(tile_value, kv_first * DH, kv_width, 0)

    def spread_heads(packed):
        five = packed.reshape(cand_count, seq_len, kv_count, 1, DH)
        return jnp.broadcast_to(five, (cand_count, seq_len, kv_count, repeats, DH)).reshape(
            cand_count, seq_len, heads_dev, DH
        )

    queries = query_act.reshape(cand_count, seq_len, heads_dev, DH)
    key_heads = spread_heads(key_local)
    value_heads = spread_heads(value_local)
    grad_heads = ctx_grad.reshape(cand_count, seq_len, heads_dev, DH)
    both_down = jnp.concatenate([down_query, down_value], axis=1)
    lowrank_part = jnp.einsum(
        "bsd,dr->bsr", hidden_in, both_down, preferred_element_type=jnp.float32
    )
    position = jnp.arange(seq_len, dtype=jnp.int32)
    allowed = (position[None, :] <= position[:, None])[None] & (
        segment_ids[:, :, None] == segment_ids[:, None, :]
    )
    score_scale = 1.0 / math.sqrt(DH)
    logits = (
        jnp.einsum("bqhd,bkhd->bhqk", queries, key_heads, preferred_element_type=jnp.float32)
        * score_scale
    )
    logits = jnp.where(allowed[:, None], logits, -1e30)
    row_top = jnp.max(logits, axis=-1, keepdims=True)
    exp_terms = jnp.exp(logits - row_top)
    attn_probs = exp_terms / jnp.sum(exp_terms, axis=-1, keepdims=True)
    value_grad = jnp.einsum(
        "bhqk,bqhd->bkhd",
        attn_probs.astype(jnp.bfloat16),
        grad_heads,
        preferred_element_type=jnp.float32,
    ).astype(jnp.bfloat16)
    prob_grad = jnp.einsum(
        "bqhd,bkhd->bhqk", grad_heads, value_heads, preferred_element_type=jnp.float32
    )
    row_delta = jnp.sum(attn_probs * prob_grad, axis=-1, keepdims=True)
    logit_grad = (attn_probs * (prob_grad - row_delta)).astype(jnp.bfloat16)
    query_grad = (
        jnp.einsum("bhqk,bkhd->bqhd", logit_grad, key_heads, preferred_element_type=jnp.float32)
        * score_scale
    )
    query_grad = query_grad.astype(jnp.bfloat16).reshape(cand_count, seq_len, width_dev)
    value_five = value_grad.reshape(cand_count, seq_len, kv_count, repeats, DH)
    up_three = up_local.reshape(R, kv_count, DH)
    back_query = jnp.einsum("bsc,rc->bsr", query_grad, up_query, preferred_element_type=jnp.float32)
    back_value = jnp.einsum(
        "bskgd,rkd->bsr", value_five, up_three, preferred_element_type=jnp.float32
    )
    back_part = jnp.concatenate([back_query, back_value], axis=2)
    lowrank_in, lowrank_back = lax.psum((lowrank_part, back_part), "mp")
    lowrank_in = lowrank_in.astype(jnp.bfloat16)
    lowrank_back = lowrank_back.astype(jnp.bfloat16)
    grad_down = jnp.einsum(
        "bsd,bsr->bdr", hidden_in, lowrank_back, preferred_element_type=jnp.float32
    )
    grad_upq = jnp.einsum(
        "bsr,bsc->bcr", lowrank_in[:, :, :R], query_grad, preferred_element_type=jnp.float32
    )
    grad_upv = jnp.einsum(
        "bsr,bskgd->bkdr", lowrank_in[:, :, R:], value_five, preferred_element_type=jnp.float32
    )
    grad_upv = grad_upv.reshape(cand_count, kv_width, R)
    grad_rows = jnp.concatenate(
        [grad_down[:, :, :R], grad_down[:, :, R:], grad_upq, grad_upv], axis=1
    )
    bucket_ids = jnp.concatenate(
        [(block_rows * NT + tile_rows).reshape(-1), block_local * NT + tile_local]
    )
    out_blocks = K // PB
    block_sums = jax.ops.segment_sum(
        jnp.moveaxis(grad_rows, 1, 0), bucket_ids, num_segments=out_blocks * NT
    )
    block_sums = (
        block_sums.reshape(out_blocks, NT, cand_count, R)
        .transpose(2, 0, 1, 3)
        .reshape(cand_count, out_blocks, NT * R)
    )
    tile_table = tile_bank.astype(jnp.float32).reshape(NT * R, PB)
    projected = jnp.einsum(
        "bkj,jp->bkp", block_sums, tile_table, precision=lax.Precision.HIGHEST
    ).reshape(cand_count, K)
    feat_slice = lax.psum_scatter(
        projected.astype(jnp.bfloat16), "mp", scatter_dimension=1, tiled=True
    ).astype(jnp.float32)
    feat_square = jnp.sum(feat_slice * feat_slice, axis=1)
    feat_half = feat_slice.astype(jnp.bfloat16)
    partial_value = jnp.einsum(
        "bk,sk->bs",
        feat_half,
        lax.all_gather(seed_feats, "dp", axis=0, tiled=True),
        preferred_element_type=jnp.float32,
    )
    total_square = lax.psum(feat_square, "mp")
    numerator = lax.psum_scatter(partial_value, "mp", scatter_dimension=1, tiled=True)
    return numerator * lax.rsqrt(total_square / K + EPS)[:, None] * K ** (-0.5)


def solution(mesh):
    return jax.shard_map(
        local,
        mesh=mesh,
        in_specs=(
            P("dp", None, "mp"),
            P("dp", None, "mp"),
            P("dp", None, None),
            P("dp", None, None),
            P("dp", None, "mp"),
            P("dp", None),
            P("mp", None),
            P(None, "mp"),
            P("mp", None),
            P(),
            P(None, "mp"),
            P(None, "mp"),
            P(),
            P(),
            P(),
            P("dp", "mp"),
        ),
        out_specs=P("dp", "mp"),
        check_vma=False,
    )
```

profile of v0, /device:TPU:2, one launch (start us, length us, event | category | flops | bytes accessed | tf_op | source)
XLA Modules:
  0.0 423.8 jit_solution(10338486193786208510)
XLA Ops:
  7.5 1.1 constant_dynamic-slice_fusion
  8.7 2.5 fusion.22
  11.2 0.4 compare_and_fusion
  11.7 6.1 %fusion.55 = (f32[2,4,512]{2,1,0:T(4,128)S(1)}, f32[2,4,512,512]{2,3,1,0:T(8,128)}) fusion(f32[2,4,512,512]{3,2,1,0:T(8,128)S(1)} %fusion.22, pred[2,512,512]{1,2,0:T(8,128)(4,1)S(1)} %compare_and_fusion), kind=kOutput, calls=%fused_computation.71 | output fusion | flops 12583423 | bytes 17317888 | tf_op jit(solution)/shard_map/sub | solution.py:74
  17.8 4.8 %convert_reduce_fusion = bf16[2,512,128]{2,1,0:T(8,128)(2,1)S(1)} fusion(f32[2,4,512,512]{2,3,1,0:T(8,128)} %get-tuple-element.10, f32[2,4,512]{2,1,0:T(4,128)S(1)} %get-tuple-element.9, bf16[2,512,512]{2,1,0:T(8,128)(2,1)S(1)} %copy-done), kind=kOutput, calls=%fused_computation.18 | convolution fusion | flops 542507008 | bytes 9715712 | tf_op jit(solution)/shard_map/bhqk,bqhd->bkhd/dot_general | solution.py:76
  22.6 1.0 copy-done.9
  23.5 1.5 fusion.1
  25.1 1.6 multiply_convert_fusion
  26.7 0.3 fusion.44
  27.0 1.0 fusion.46
  28.0 1.1 pad_maximum_fusion
  29.1 1.0 copy.37
  30.1 1.7 copy.38
  31.7 2.4 convolution_bitcast_fusion
  34.2 89.1 %all-reduce.2 = (bf16[2,512,256]{1,2,0:T(8,128)(2,1)}, bf16[2,512,256]{1,2,0:T(8,128)(2,1)}) all-reduce(f32[2,512,256]{1,2,0:T(8,128)} %convolution_bitcast_fusion, f32[2,512,256]{1,2,0:T(8,128)} %pad_maximum_fusion), channel_id=1, replica_groups=mesh['dp'=32,'mp'=16] {'mp'}, use_global_device_ids=true, to_apply=%region_5.6 | all-reduce | flops 524288 | bytes 3145728 | tf_op jit(solution)/shard_map/psum | solution.py:99
  123.2 1.4 fusion.39
  124.7 1.2 fusion.37
  125.9 1.5 convolution_bitcast_fusion.1
  127.5 1.3 maximum_bitcast_fusion
  128.8 3.2 copy.44
  132.0 0.8 dynamic-slice_add_fusion
  133.0 60.1 %scatter_fusion = f32[512,2,128]{2,1,0:T(2,128)S(1)} fusion(f32[512,2,128]{2,1,0:T(2,128)S(1)} %broadcast_in_dim.12, s32[1664]{0:T(1024)S(1)} %pad_add_fusion, f32[1664,2,128]{2,1,0:T(2,128)S(1)} %copy.44), kind=kCustom, calls=%fused_computation | custom fusion | flops 425984 | bytes 5118464 | tf_op jit(solution)/shard_map/scatter-add | solution.py:119
  193.1 0.5 fusion.18
  193.6 1.9 copy.58
  195.6 0.5 all-gather.2.cloned.1.call-update
  196.1 92.7 %reduce-scatter.7.cloned.1.call-done = bf16[512,2]{1,0:T(8,128)(2,1)} async-done(((bf16[8192,2]{1,0:T(8,128)(2,1)}), bf16[512,2]{1,0:T(8,128)(2,1)}) %reduce-scatter.7.cloned.1.call-update) | async-done | bytes 2064
  288.8 1.0 copy.55
  289.9 33.3 %psum.23 = f32[2]{0:T(128)S(1)} all-reduce(f32[2]{0:T(128)S(1)} %multiply_reduce_fusion), channel_id=1, replica_groups=mesh['dp'=32,'mp'=16] {'mp'}, use_global_device_ids=true, to_apply=%region_10.11 | all-reduce | flops 2 | bytes 16 | tf_op jit(solution)/shard_map/psum | solution.py:142
  323.2 2.5 convolution_bitcast_fusion.2
  325.8 89.1 %reduce-scatter.9.cloned.1.call-done = f32[64,2]{1,0:T(8,128)} async-done(((f32[1024,2]{1,0:T(8,128)}), f32[64,2]{1,0:T(8,128)}) %reduce-scatter.9.cloned.1.call-update) | async-done | bytes 528
  414.9 0.8 copy.57
  415.7 0.6 multiply_multiply_fusion
  (34 shorter events, 0.8 us)
Async XLA Ops:
  7.4 10.4 %copy-start = (bf16[2,512,512]{2,1,0:T(8,128)(2,1)S(1)}, bf16[2,512,512]{2,1,0:T(8,128)(2,1)}, u32[]{:S(2)}) copy-start(bf16[2,512,512]{2,1,0:T(8,128)(2,1)} %param.20) | copy-start | bytes 3145732
  7.4 3.9 copy-start.6
  7.4 281.4 %reduce-scatter.7.cloned.1.call-start = ((), (), s32[]{:S(2)}) async-start(), calls=%async_computation.3 | async-start | bytes 2228224
  17.8 5.8 %copy-start.9 = (f32[2,4,512,512]{2,3,1,0:T(8,128)S(1)}, f32[2,4,512,512]{2,3,1,0:T(8,128)}, u32[]{:S(2)}) copy-start(f32[2,4,512,512]{2,3,1,0:T(8,128)} %get-tuple-element.10) | copy-start | bytes 25165828
  22.6 4.4 %copy-start.2 = (bf16[2,512,128]{2,1,0:T(8,128)(2,1)}, bf16[2,512,128]{2,1,0:T(8,128)(2,1)S(1)}, u32[]{:S(2)}) copy-start(bf16[2,512,128]{2,1,0:T(8,128)(2,1)S(1)} %convert_reduce_fusion) | copy-start | bytes 786436
  25.0 1.6 copy-start.5
  25.1 6.7 %copy-start.1 = (bf16[2,512,512]{2,1,0:T(8,128)(2,1)S(1)}, bf16[2,512,512]{2,1,0:T(8,128)(2,1)}, u32[]{:S(2)}) copy-start(bf16[2,512,512]{2,1,0:T(8,128)(2,1)} %param.16) | copy-start | bytes 3145732
  28.0 96.7 %copy-start.3 = (bf16[2,512,128]{2,1,0:T(8,128)(2,1)S(1)}, bf16[2,512,128]{2,1,0:T(8,128)(2,1)}, u32[]{:S(2)}) copy-start(bf16[2,512,128]{2,1,0:T(8,128)(2,1)} %copy-done.2) | copy-start | bytes 786436
  34.1 97.9 %copy-start.7 = (s32[3,512]{1,0:T(4,128)S(1)}, s32[3,512]{1,0:T(4,128)}, u32[]{:S(2)}) copy-start(s32[3,512]{1,0:T(4,128)} %param.27) | copy-start | bytes 18436
  34.2 97.9 %copy-start.8 = (s32[3,512]{1,0:T(4,128)S(1)}, s32[3,512]{1,0:T(4,128)}, u32[]{:S(2)}) copy-start(s32[3,512]{1,0:T(4,128)} %param.26) | copy-start | bytes 18436
  125.8 67.2 %copy-start.4 = (bf16[8,128,128]{2,1,0:T(8,128)(2,1)S(1)}, bf16[8,128,128]{2,1,0:T(8,128)(2,1)}, u32[]{:S(2)}) copy-start(bf16[8,128,128]{2,1,0:T(8,128)(2,1)} %param.30) | copy-start | bytes 786436
  195.5 127.7 %all-gather.2.cloned.1.call-start = ((), (), s32[]{:S(2)}) async-start(), calls=%async_computation.2 | async-start | bytes 1081344 | tf_op jit(solution)/shard_map/all_gather | solution.py:139
  196.1 218.8 %reduce-scatter.9.cloned.1.call-start = ((), (), s32[]{:S(2)}) async-start(), calls=%async_computation.4 | async-start | bytes 557056
Sparse Core Ops, SparseCore 0:
  195.6 93.1 reduce-scatter.6
  325.9 88.9 reduce-scatter.8
Sparse Core Ops, SparseCore 1:
  198.3 74.8 all-gather.1
where the time goes:
time: 424 us
  waiting for transfers between devices  182 us (43%)
  blocking collectives  122 us (29%)
  other arithmetic  70.6 us (17%)
  matrix products  21.2 us (5%)
  between operations  15.1 us (4%)
  local copies, waits for them, and re-layouts  12.1 us (3%)
    unnamed x5, waiting for transfers between devices  182 us
    psum x1, blocking collectives, local(): lowrank_in, lowrank_back = lax.psum((lowrank_part, back_part), 'mp')  89.1 us
    scatter-add x1, other arithmetic, local(): jax.ops.segment_sum(jnp.moveaxis(grad_rows, 1, 0), bucket_ids, num_segmen...  60.1 us
    psum x1, blocking collectives, local(): total_square = lax.psum(feat_square, 'mp')  33.3 us
  transfers between devices with their start and end apart: 3, of which 2 were waited for; matrix products, arithmetic and copies ran while one was open for 0% of the time, Pallas kernels for 0%

commit v1 on v0

--- a/solution.py
+++ b/solution.py
@@ -139,7 +139,7 @@
         lax.all_gather(seed_feats, "dp", axis=0, tiled=True),
         preferred_element_type=jnp.float32,
     )
-    total_square = lax.psum(feat_square, "mp")
+    total_square = jnp.sum(lax.all_gather(feat_square, "mp"), axis=0)
     numerator = lax.psum_scatter(partial_value, "mp", scatter_dimension=1, tiled=True)
     return numerator * lax.rsqrt(total_square / K + EPS)[:, None] * K ** (-0.5)
 

time: 424 us -> 425 us (level)
    psum x1 -> x0, blocking collectives: 33.3 us -> none  [local(): total_square = lax.psum(feat_square, 'mp')]
    unnamed x0 -> x1, blocking collectives: none -> 33.2 us
    unnamed x25 -> x28, local copies, waits for them, and re-layouts: 7.41 us -> 8.92 us
  transfers between devices with their start and end apart: 3 -> 3, of which waited for: 2 -> 2; matrix products, arithmetic and copies ran while one was open for 0% -> 1% of each run, Pallas kernels for 0% -> 0%
where the time goes in v1:
time: 425 us; the launch traced here: 424 us
  waiting for transfers between devices  180 us (42%)
  blocking collectives  122 us (29%)
  other arithmetic  70.6 us (17%)
  matrix products  21.2 us (5%)
  between operations  15.8 us (4%)
  local copies, waits for them, and re-layouts  13.7 us (3%)
    unnamed x5, waiting for transfers between devices  180 us
    psum x1, blocking collectives, local(): lowrank_in, lowrank_back = lax.psum((lowrank_part, back_part), 'mp')  89.1 us
    scatter-add x1, other arithmetic, local(): jax.ops.segment_sum(jnp.moveaxis(grad_rows, 1, 0), bucket_ids, num_segmen...  60.1 us
    unnamed x1, blocking collectives  33.2 us
    unnamed x28, local copies, waits for them, and re-layouts  8.92 us
  transfers between devices with their start and end apart: 3, of which 2 were waited for; matrix products, arithmetic and copies ran while one was open for 1% of the time, Pallas kernels for 0%

profile of v1, /device:TPU:2, one launch (start us, length us, event | category | flops | bytes accessed | tf_op | source)
XLA Modules:
  0.0 424.2 jit_solution(3363113316999388174)
XLA Ops:
  7.5 1.1 constant_dynamic-slice_fusion
  8.7 2.5 fusion.22
  11.2 0.4 compare_and_fusion
  11.7 6.1 %fusion.55 = (f32[2,4,512]{2,1,0:T(4,128)S(1)}, f32[2,4,512,512]{2,3,1,0:T(8,128)}) fusion(f32[2,4,512,512]{3,2,1,0:T(8,128)S(1)} %fusion.22, pred[2,512,512]{1,2,0:T(8,128)(4,1)S(1)} %compare_and_fusion), kind=kOutput, calls=%fused_computation.71 | output fusion | flops 12583423 | bytes 17317888 | tf_op jit(solution)/shard_map/sub | solution.py:74
  17.8 4.8 %convert_reduce_fusion = bf16[2,512,128]{2,1,0:T(8,128)(2,1)S(1)} fusion(f32[2,4,512,512]{2,3,1,0:T(8,128)} %get-tuple-element.10, f32[2,4,512]{2,1,0:T(4,128)S(1)} %get-tuple-element.9, bf16[2,512,512]{2,1,0:T(8,128)(2,1)S(1)} %copy-done), kind=kOutput, calls=%fused_computation.18 | convolution fusion | flops 542507008 | bytes 9715712 | tf_op jit(solution)/shard_map/bhqk,bqhd->bkhd/dot_general | solution.py:76
  22.6 1.0 copy-done.9
  23.5 1.5 fusion.1
  25.1 1.6 multiply_convert_fusion
  27.0 1.0 fusion.46
  28.0 1.1 pad_maximum_fusion
  29.1 1.0 copy.52
  30.1 1.7 copy.53
  31.7 2.4 convolution_bitcast_fusion
  34.2 89.1 %all-reduce.3 = (bf16[2,512,256]{1,2,0:T(8,128)(2,1)}, bf16[2,512,256]{1,2,0:T(8,128)(2,1)}) all-reduce(f32[2,512,256]{1,2,0:T(8,128)} %convolution_bitcast_fusion, f32[2,512,256]{1,2,0:T(8,128)} %pad_maximum_fusion), channel_id=1, replica_groups=mesh['dp'=32,'mp'=16] {'mp'}, use_global_device_ids=true, to_apply=%region_5.6 | all-reduce | flops 524288 | bytes 3145728 | tf_op jit(solution)/shard_map/psum | solution.py:99
  123.2 1.4 fusion.39
  124.7 1.2 fusion.37
  125.9 1.5 convolution_bitcast_fusion.1
  127.5 1.3 maximum_bitcast_fusion
  128.8 3.2 copy.59
  132.0 0.8 dynamic-slice_add_fusion
  133.0 60.1 %scatter_fusion = f32[512,2,128]{2,1,0:T(2,128)S(1)} fusion(f32[512,2,128]{2,1,0:T(2,128)S(1)} %broadcast_in_dim.12, s32[1664]{0:T(1024)S(1)} %pad_add_fusion, f32[1664,2,128]{2,1,0:T(2,128)S(1)} %copy.59), kind=kCustom, calls=%fused_computation | custom fusion | flops 425984 | bytes 5118464 | tf_op jit(solution)/shard_map/scatter-add | solution.py:119
  193.1 0.5 fusion.18
  193.6 1.9 copy.74
  195.6 0.5 all-gather.3.cloned.1.call-update
  196.1 1.3 dynamic-slice
  198.1 90.7 %reduce-scatter.7.cloned.1.call-done = bf16[512,2]{1,0:T(8,128)(2,1)} async-done(((bf16[8192,2]{1,0:T(8,128)(2,1)}), bf16[512,2]{1,0:T(8,128)(2,1)}) %reduce-scatter.7.cloned.1.call-update) | async-done | bytes 2064
  288.8 1.0 copy.71
  290.2 33.2 %all-reduce = f32[32]{0:T(128)S(1)} all-reduce(f32[32]{0:T(128)S(1)} %dynamic-update-slice), channel_id=2, replica_groups=mesh['dp'=32,'mp'=16] {'mp'}, use_global_device_ids=true, to_apply=%add | all-reduce | flops 32 | bytes 256
  323.6 2.5 convolution_bitcast_fusion.2
  326.1 89.1 %reduce-scatter.9.cloned.1.call-done = f32[64,2]{1,0:T(8,128)} async-done(((f32[1024,2]{1,0:T(8,128)}), f32[64,2]{1,0:T(8,128)}) %reduce-scatter.9.cloned.1.call-update) | async-done | bytes 528
  415.3 0.8 copy.73
  416.1 0.6 multiply_multiply_fusion
  (39 shorter events, 1.4 us)
Async XLA Ops:
  7.4 10.4 %copy-start = (bf16[2,512,512]{2,1,0:T(8,128)(2,1)S(1)}, bf16[2,512,512]{2,1,0:T(8,128)(2,1)}, u32[]{:S(2)}) copy-start(bf16[2,512,512]{2,1,0:T(8,128)(2,1)} %param.20) | copy-start | bytes 3145732
  7.4 3.9 copy-start.6
  7.4 281.4 %reduce-scatter.7.cloned.1.call-start = ((), (), s32[]{:S(2)}) async-start(), calls=%async_computation.3 | async-start | bytes 2228224
  17.8 5.8 %copy-start.9 = (f32[2,4,512,512]{2,3,1,0:T(8,128)S(1)}, f32[2,4,512,512]{2,3,1,0:T(8,128)}, u32[]{:S(2)}) copy-start(f32[2,4,512,512]{2,3,1,0:T(8,128)} %get-tuple-element.10) | copy-start | bytes 25165828
  22.6 4.4 %copy-start.2 = (bf16[2,512,128]{2,1,0:T(8,128)(2,1)}, bf16[2,512,128]{2,1,0:T(8,128)(2,1)S(1)}, u32[]{:S(2)}) copy-start(bf16[2,512,128]{2,1,0:T(8,128)(2,1)S(1)} %convert_reduce_fusion) | copy-start | bytes 786436
  25.0 1.6 copy-start.5
  25.1 6.7 %copy-start.1 = (bf16[2,512,512]{2,1,0:T(8,128)(2,1)S(1)}, bf16[2,512,512]{2,1,0:T(8,128)(2,1)}, u32[]{:S(2)}) copy-start(bf16[2,512,512]{2,1,0:T(8,128)(2,1)} %param.16) | copy-start | bytes 3145732
  28.0 96.7 %copy-start.3 = (bf16[2,512,128]{2,1,0:T(8,128)(2,1)S(1)}, bf16[2,512,128]{2,1,0:T(8,128)(2,1)}, u32[]{:S(2)}) copy-start(bf16[2,512,128]{2,1,0:T(8,128)(2,1)} %copy-done.2) | copy-start | bytes 786436
  34.1 97.9 %copy-start.7 = (s32[3,512]{1,0:T(4,128)S(1)}, s32[3,512]{1,0:T(4,128)}, u32[]{:S(2)}) copy-start(s32[3,512]{1,0:T(4,128)} %param.27) | copy-start | bytes 18436
  34.2 97.9 %copy-start.8 = (s32[3,512]{1,0:T(4,128)S(1)}, s32[3,512]{1,0:T(4,128)}, u32[]{:S(2)}) copy-start(s32[3,512]{1,0:T(4,128)} %param.26) | copy-start | bytes 18436
  125.8 67.2 %copy-start.4 = (bf16[8,128,128]{2,1,0:T(8,128)(2,1)S(1)}, bf16[8,128,128]{2,1,0:T(8,128)(2,1)}, u32[]{:S(2)}) copy-start(bf16[8,128,128]{2,1,0:T(8,128)(2,1)} %param.30) | copy-start | bytes 786436
  195.5 128.0 %all-gather.3.cloned.1.call-start = ((), (), s32[]{:S(2)}) async-start(), calls=%async_computation.2 | async-start | bytes 1081344 | tf_op jit(solution)/shard_map/all_gather | solution.py:139
  196.1 219.2 %reduce-scatter.9.cloned.1.call-start = ((), (), s32[]{:S(2)}) async-start(), calls=%async_computation.4 | async-start | bytes 557056
Sparse Core Ops, SparseCore 0:
  195.6 93.1 reduce-scatter.6
  326.2 88.9 reduce-scatter.8
Sparse Core Ops, SparseCore 1:
  198.3 74.8 all-gather.2
